TPU v7x, 32 devices: a whole 2x2x4 slice. The times are simulated.
32 devices in a mesh: expert: 8 (over y, x, core), token: 4 (over z).
Axes of the slice: x: 2, y: 2, z: 4, core: 2. Of those that a mesh axis runs over, the one named last changes fastest.
Arguments:
- activations: bfloat16 [16, 1024, 768], P('expert', 'token'), may hold values from -6 to 6
- routed: int32 [16, 1024], P('expert', 'token'), may hold values 0 or 1
- weights: bfloat16 [128, 768, 256], P(('expert', 'token')), may hold values from -6 to 6, as said below
- kept_mask: int32 [128, 768, 256], P(('expert', 'token')), may hold values 0 or 1
- step_counts: int32 [128], P(('expert', 'token')), may hold values from 1 to 7
- ridge_scale: float32 [128], P(('expert', 'token')), may hold values from 0.05 to 0.5
Outputs:
- rebuilt: float32 [128, 768, 256], P(('expert', 'token'))
- misfit: float32 [16], P('expert')
Inputs may be any that keep to these rules, and one draw needn't show every extreme that they name: `weights`: every entry's magnitude is at least 0.25.
All inputs are finite; a program needn't handle non-finite values. No bound on the sum of `routed` or of `kept_mask` on one device may be relied on, other than what follows from the above.
Results may differ from a plain program's by a relative error of at most 0.0003.
Values may be sent and summed in bfloat16 or wider, within the bound.
A program may use at most 64 MiB of HBM per device.

v0:
```python
import functools

import jax
import jax.numpy as jnp
from jax import lax
from jax.experimental import pallas as pl
from jax.experimental.pallas import tpu as pltpu
from jax.sharding import PartitionSpec as P

D = 2048
COLS = 256
MESH = pl.DeviceIdType.MESH


def dot(a, b):
    return jnp.dot(a, b, preferred_element_type=jnp.float32)


def split(value):
    high = value.astype(jnp.bfloat16)
    return high, (value - high.astype(jnp.float32)).astype(jnp.bfloat16)


def gram_kernel(
    tokens, group, x_ref, routed_ref, w_hbm, high_ref, low_ref, stats_ref,
    recv, own_rows, routes, total, outer, w_buf, own_sem, w_sem, send_sem, recv_sem, route_send, route_recv,
):
    slots, rows, features = x_ref.shape
    block = features // 3 if features % 384 == 0 else features
    me = lax.axis_index("token")
    own = me // group
    load_rows = pltpu.make_async_copy(x_ref.at[own], own_rows, own_sem)
    load_rows.start()
    load = pltpu.make_async_copy(w_hbm, w_buf, w_sem)
    load.start()

    has_left = me > 0
    has_right = me < tokens - 1
    barrier = pltpu.get_barrier_semaphore()

    @pl.loop(1, tokens)
    def _(offset):
        pl.semaphore_signal(
            barrier, inc=1, device_id={"token": lax.rem(me + offset, tokens)}, device_id_type=MESH
        )

    pl.semaphore_wait(barrier, tokens - 1)

    def route_copy(offset):
        return pltpu.make_async_remote_copy(
            src_ref=routed_ref,
            dst_ref=routes.at[me],
            send_sem=route_send.at[offset],
            recv_sem=route_recv.at[offset],
            device_id={"token": lax.rem(me + offset, tokens)},
            device_id_type=MESH,
        )

    def sends(way, k, slot):
        if way == 0:
            return has_right & (me - k >= 0) & ((slot + 1) * group - 1 >= me + 1)
        return has_left & (me + k < tokens) & (slot * group <= me - 1)

    def receives(way, k, slot):
        if way == 0:
            return (me - 1 - k >= 0) & ((slot + 1) * group - 1 >= me)
        return (me + 1 + k < tokens) & (slot * group <= me)

    def copy(way, k, slot, source, origin):
        return pltpu.make_async_remote_copy(
            src_ref=source,
            dst_ref=recv.at[slot, origin],
            send_sem=send_sem.at[way, k, slot],
            recv_sem=recv_sem.at[way, k, slot],
            device_id={"token": me + 1 if way == 0 else me - 1},
            device_id_type=MESH,
        )

    def slot_order(way):
        return range(slots - 1, -1, -1) if way == 0 else range(slots)

    def add_gram(rows_ref, route):
        value = rows_ref[...]
        left = value.T * route.astype(jnp.float32).astype(jnp.bfloat16)
        for start in range(0, features, block):
            total[start : start + block, :] += dot(left[start : start + block, :], value)

    for place in range(slots):
        for way in range(2):
            slot = list(slot_order(way))[place]

            @pl.when(sends(way, 0, slot))
            def _(way=way, slot=slot):
                copy(way, 0, slot, x_ref.at[slot], me).start()

        if place == 0:

            @pl.loop(1, tokens)
            def _(offset):
                route_copy(offset).start()

    total[...] = jnp.zeros_like(total)
    load_rows.wait()
    add_gram(own_rows, routed_ref[pl.ds(own, 1), :])
    outer[...] = jnp.zeros_like(outer)
    load.wait()

    @pl.loop(0, w_buf.shape[0])
    def _(task):
        value = w_buf[task]
        for start in range(0, features, block):
            outer[start : start + block, :] += lax.dot_general(
                value[start : start + block, :], value, (((1,), (1,)), ((), ())),
                preferred_element_type=jnp.float32,
            )

    @pl.loop(1, tokens)
    def _(offset):
        route_copy(offset).wait_recv()

    def origin_of(way, k):
        return me - 1 - k if way == 0 else me + 1 + k

    @pl.loop(0, tokens - 1)
    def _(k):
        for place in range(slots):
            for way in range(2):
                slot = list(slot_order(way))[place]
                origin = origin_of(way, k)

                @pl.when(sends(way, k + 1, slot))
                def _(way=way, slot=slot, origin=origin):
                    copy(way, k, slot, x_ref.at[slot], origin).wait_recv()
                    copy(way, k + 1, slot, recv.at[slot, origin], origin).start()

        for way in range(2):

            @pl.when(sends(way, k + 1, own))
            def _(way=way):
                origin = origin_of(way, k)
                add_gram(recv.at[own, origin], routes[origin, pl.ds(own, 1), :])

    @pl.loop(0, tokens - 1)
    def _(k):
        for way in range(2):

            @pl.when(receives(way, k, own) & jnp.logical_not(sends(way, k + 1, own)))
            def _(way=way):
                origin = origin_of(way, k)
                copy(way, k, own, x_ref.at[own], origin).wait_recv()
                add_gram(recv.at[own, origin], routes[origin, pl.ds(own, 1), :])

    scale = 1.0 / (rows * tokens)
    square = jnp.zeros((1, features), jnp.float32)
    energy = jnp.zeros((1, features), jnp.float32)
    piece = block // 4
    for start in range(0, features, piece):
        part = total[start : start + piece, :] * scale
        high, low = split(part)
        high_ref[start : start + piece, :] = high
        low_ref[start : start + piece, :] = low
        square = square + jnp.sum(part * part, axis=0, keepdims=True)
        energy = energy + jnp.sum(part * outer[start : start + piece, :], axis=0, keepdims=True)
    stats_ref[0] = jnp.sum(square)
    stats_ref[1] = jnp.sum(energy)

    @pl.loop(0, tokens - 1)
    def _(k):
        for way in range(2):
            for slot in range(slots):

                @pl.when(sends(way, k, slot))
                def _(way=way, slot=slot):
                    copy(way, k, slot, x_ref.at[slot], me).wait_send()

    @pl.loop(1, tokens)
    def _(offset):
        route_copy(offset).wait_send()


def gram_call(tokens, group, activations, routed, weights):
    slots, rows, features = activations.shape
    vmem = pl.BlockSpec(memory_space=pltpu.VMEM)
    hops = max(tokens, 2)
    hbm = pl.BlockSpec(memory_space=pltpu.HBM)
    return pl.pallas_call(
        functools.partial(gram_kernel, tokens, group),
        out_shape=(
            jax.ShapeDtypeStruct((features, features), jnp.bfloat16),
            jax.ShapeDtypeStruct((features, features), jnp.bfloat16),
            jax.ShapeDtypeStruct((2,), jnp.float32),
        ),
        in_specs=[hbm, vmem, hbm],
        out_specs=(vmem, vmem, pl.BlockSpec(memory_space=pltpu.SMEM)),
        scratch_shapes=[
            pltpu.VMEM((slots, tokens, rows, features), jnp.bfloat16),
            pltpu.VMEM((rows, features), jnp.bfloat16),
            pltpu.VMEM((tokens, slots, rows), jnp.int32),
            pltpu.VMEM((features, features), jnp.float32),
            pltpu.VMEM((features, features), jnp.float32),
            pltpu.VMEM(weights.shape, weights.dtype),
            pltpu.SemaphoreType.DMA,
            pltpu.SemaphoreType.DMA,
            pltpu.SemaphoreType.DMA((2, hops, slots)),
            pltpu.SemaphoreType.DMA((2, hops, slots)),
            pltpu.SemaphoreType.DMA((hops,)),
            pltpu.SemaphoreType.DMA((hops,)),
        ],
        compiler_params=pltpu.CompilerParams(
            collective_id=0, has_side_effects=True, vmem_limit_bytes=62 << 20
        ),
    )(activations, routed, weights)


def solve_kernel(
    group, counts_ref, ridge_ref, stats_ref, high_ref, low_ref, w_ref, mask_ref,
    out_ref, payload_ref, delta, change, pending, cross,
):
    task = pl.program_id(0)
    features, columns = delta.shape
    block = features // 3 if features % 384 == 0 else features
    starts = range(0, features, block)
    row = (1, columns)
    frobenius = jnp.sqrt(jnp.full(row, stats_ref[0], jnp.float32))
    damping = ridge_ref[task] * frobenius
    step = 1.0 / (frobenius + damping)
    shrink = step * damping

    def times_gram(at, right):
        return dot(high_ref[at, :], right) + dot(low_ref[at, :], right)

    pruned = jnp.where(mask_ref[0] == 0, w_ref[0], jnp.zeros_like(w_ref[0]))
    for start in starts:
        at = slice(start, start + block)
        product = times_gram(at, pruned)
        cross[at, :] = product
        begin = jnp.where(
            mask_ref[0, at, :] != 0,
            step * product - shrink * w_ref[0, at, :].astype(jnp.float32),
            0.0,
        )
        delta[at, :] = begin
        change[at, :] = begin
        pending[at, :] = begin

    @pl.loop(1, counts_ref[task])
    def _(turn):
        right = pending[...].astype(jnp.bfloat16)
        for start in starts:
            at = slice(start, start + block)
            product = times_gram(at, right)
            left_out = pending[at, :] - right[at, :].astype(jnp.float32)
            fresh = (1.0 - shrink) * delta[at, :] - jnp.where(
                mask_ref[0, at, :] != 0, step * product, 0.0
            )
            delta[at, :] = fresh
            change[at, :] += fresh
            pending[at, :] = fresh + left_out

    right_high, right_low = split(change[...])
    numerator = jnp.zeros(row, jnp.float32)
    for start in starts:
        at = slice(start, start + block)
        product = times_gram(at, right_high) + dot(high_ref[at, :], right_low)
        weight = w_ref[0, at, :].astype(jnp.float32)
        kept = mask_ref[0, at, :] != 0
        out_ref[0, at, :] = change[at, :] + jnp.where(kept, weight, 0.0)
        numerator = numerator + jnp.sum(
            (change[at, :] - jnp.where(kept, 0.0, weight)) * (product - cross[at, :]),
            axis=0, keepdims=True,
        )

    own = lax.axis_index("token") // group
    lanes = lax.broadcasted_iota(jnp.int32, payload_ref.shape, 1)
    lines = lax.broadcasted_iota(jnp.int32, payload_ref.shape, 0)

    @pl.when(task == 0)
    def _():
        payload_ref[...] = jnp.where(lines == 0, stats_ref[1], 0.0)

    payload_ref[...] += jnp.where((lines == 1) & (lanes == own), jnp.sum(numerator), 0.0)


def solve_call(group, counts, ridge, stats, high, low, weights, mask):
    tasks, features, columns = weights.shape
    smem = pl.BlockSpec(memory_space=pltpu.SMEM)
    vmem = pl.BlockSpec(memory_space=pltpu.VMEM)
    item = pl.BlockSpec((1, features, columns), lambda i: (i, 0, 0))
    plane = pltpu.VMEM((features, columns), jnp.float32)
    return pl.pallas_call(
        functools.partial(solve_kernel, group),
        grid=(tasks,),
        out_shape=(
            jax.ShapeDtypeStruct(weights.shape, jnp.float32),
            jax.ShapeDtypeStruct((8, 128), jnp.float32),
        ),
        in_specs=[smem, smem, smem, vmem, vmem, item, item],
        out_specs=(item, pl.BlockSpec((8, 128), lambda i: (0, 0))),
        scratch_shapes=[plane, plane, plane, plane],
        compiler_params=pltpu.CompilerParams(vmem_limit_bytes=62 << 20),
    )(counts, ridge, stats, high, low, weights, mask)


def misfit_kernel(experts, tokens, slots, payload_ref, out_ref, held, send_sem, recv_sem):
    devices = experts * tokens
    expert, token = lax.axis_index("expert"), lax.axis_index("token")
    me = expert * tokens + token
    barrier = pltpu.get_barrier_semaphore()

    def peer_of(offset):
        peer = lax.rem(me + offset, devices)
        return (lax.div(peer, tokens), lax.rem(peer, tokens))

    @pl.loop(1, devices)
    def _(offset):
        pl.semaphore_signal(barrier, inc=1, device_id=peer_of(offset), device_id_type=MESH)

    pl.semaphore_wait(barrier, devices - 1)

    def copy(offset):
        return pltpu.make_async_remote_copy(
            src_ref=payload_ref,
            dst_ref=held.at[me],
            send_sem=send_sem.at[offset],
            recv_sem=recv_sem.at[offset],
            device_id=peer_of(offset),
            device_id_type=MESH,
        )

    @pl.loop(1, devices)
    def _(offset):
        copy(offset).start()

    held[me] = payload_ref[...]

    @pl.loop(1, devices)
    def _(offset):
        copy(offset).wait_recv()

    energy = jnp.sum(held[...], axis=0)[0:1, :]
    numerator = jnp.sum(held[pl.ds(expert * tokens, tokens)], axis=0)[1:2, :]
    out_ref[...] = numerator / (energy / (slots * experts) + 1e-06)

    @pl.loop(1, devices)
    def _(offset):
        copy(offset).wait_send()


def misfit_call(experts, tokens, slots, payload):
    devices = experts * tokens
    vmem = pl.BlockSpec(memory_space=pltpu.VMEM)
    return pl.pallas_call(
        functools.partial(misfit_kernel, experts, tokens, slots),
        out_shape=jax.ShapeDtypeStruct((1, 128), jnp.float32),
        in_specs=[vmem],
        out_specs=vmem,
        scratch_shapes=[
            pltpu.VMEM((devices, 8, 128), jnp.float32),
            pltpu.SemaphoreType.DMA((devices,)),
            pltpu.SemaphoreType.DMA((devices,)),
        ],
        compiler_params=pltpu.CompilerParams(collective_id=1, has_side_effects=True),
    )(payload)


def on_device(experts, tokens, activations, routed, weights, kept_mask, step_counts, ridge_scale):
    slots = activations.shape[0]
    group = (D // COLS) // weights.shape[0]
    high, low, stats = gram_call(tokens, group, activations, routed, weights)
    rebuilt, payload = solve_call(
        group, step_counts, ridge_scale, stats, high, low, weights, kept_mask
    )
    misfit = misfit_call(experts, tokens, slots, payload)[0, :slots]
    return (rebuilt, misfit)


def solution(mesh):
    placed = (
        P("expert", "token", None),
        P("expert", "token"),
        P(("expert", "token"), None, None),
        P(("expert", "token"), None, None),
        P(("expert", "token")),
        P(("expert", "token")),
    )
    return jax.shard_map(
        functools.partial(on_device, mesh.shape["expert"], mesh.shape["token"]),
        mesh=mesh,
        in_specs=placed,
        out_specs=(P(("expert", "token"), None, None), P("expert")),
        check_vma=False,
    )
```

profile of v0, /device:TPU:0, one launch (start us, length us, event | category | flops | bytes accessed | tf_op | source)
XLA Modules:
  0.0 75.2 jit_solution(8980957328445769696)
XLA Ops:
  0.6 37.0 %shard_map.77 = (bf16[768,768]{1,0:T(8,128)(2,1)}, bf16[768,768]{1,0:T(8,128)(2,1)}, f32[2]{0:T(128)}) custom-call(bf16[2,256,768]{2,1,0:T(8,128)(2,1)} %x_ref.1, s32[2,256]{1,0:T(2,128)} %routed_ref.1, bf16[4,768,256]{2,1,0:T(8,128)(2,1)} %w_ref.1), custom_call_target="tpu_custom_call" | custom-call | tf_op jit(solution)/shard_map/pallas_call | solution.py:186
  37.6 26.6 %shard_map.78 = (f32[4,768,256]{2,1,0:T(8,128)}, f32[8,128]{1,0:T(8,128)}) custom-call(s32[4]{0:T(128)} %counts_ref.1, f32[4]{0:T(128)} %ridge_ref.1, f32[2]{0:T(128)} %get-tuple-element.7.stats_ref, bf16[768,768]{1,0:T(8,128)(2,1)} %get-tuple-element.8.high_ref, bf16[768,768]{1,0:T(8,128)(2,1)} %get-tuple-element.9.low_ref, bf16[4,768,256]{2,1,0:T(8,128)(2,1)} %w_ref.1, ...), custom_call_target="tpu_custom_call" | custom-call | tf_op jit(solution)/shard_map/pallas_call | solution.py:290
  64.3 9.8 %shard_map.79 = f32[1,128]{1,0:T(1,128)} custom-call(f32[8,128]{1,0:T(8,128)} %get-tuple-element.11.payload_ref), custom_call_target="tpu_custom_call" | custom-call | tf_op jit(solution)/shard_map/pallas_call | solution.py:352
  74.1 1.1 %slice_bitcast_fusion = f32[2]{0:T(128)} fusion(f32[1,128]{1,0:T(1,128)} %shard_map.79), kind=kLoop, calls=%fused_computation | loop fusion | bytes 16 | tf_op jit(solution)/shard_map/squeeze | solution.py:373
where the time goes:
time: 76 us; the launch traced here: 75.2 us
  Pallas kernels  73.4 us (97%)
  local copies, waits for them, and re-layouts  1.14 us (1%)
    pallas_call x1, Pallas kernels, gram_call(): pl.pallas_call(functools.partial(gram_kernel, tokens, group), out_shape=(...  37 us
    pallas_call x1, Pallas kernels, solve_call(): pl.pallas_call(functools.partial(solve_kernel, group), grid=(tasks,), out...  26.6 us
    pallas_call x1, Pallas kernels, misfit_call(): pl.pallas_call(functools.partial(misfit_kernel, experts, tokens, slots),...  9.82 us

commit v1 on v0

--- a/solution.py
+++ b/solution.py
@@ -297,7 +297,7 @@
         in_specs=[smem, smem, smem, vmem, vmem, item, item],
         out_specs=(item, pl.BlockSpec((8, 128), lambda i: (0, 0))),
         scratch_shapes=[plane, plane, plane, plane],
-        compiler_params=pltpu.CompilerParams(vmem_limit_bytes=62 << 20),
+        compiler_params=pltpu.CompilerParams(vmem_limit_bytes=48 << 20),
     )(counts, ridge, stats, high, low, weights, mask)
 
 

time: 76 us -> 78.7 us (1.036); the launches traced: 75.2 us -> 79.4 us
  local copies, waits for them, and re-layouts: 1.14 us -> 4.99 us
    pallas_call x1, Pallas kernels: 9.82 us -> 19.4 us  [misfit_call(): pl.pallas_call(functools.partial(misfit_kernel, experts, tokens, slots),...]
    pallas_call x1, Pallas kernels: 26.6 us -> 17.2 us  [solve_call(): pl.pallas_call(functools.partial(solve_kernel, group), grid=(tasks,), out...]
    unnamed x0 -> x14, local copies, waits for them, and re-layouts: none -> 3.82 us
where the time goes in v1:
time: 78.7 us; the launch traced here: 79.4 us
  Pallas kernels  73.7 us (94%)
  local copies, waits for them, and re-layouts  4.99 us (6%)
    pallas_call x1, Pallas kernels, gram_call(): pl.pallas_call(functools.partial(gram_kernel, tokens, group), out_shape=(...  37.1 us
    pallas_call x1, Pallas kernels, misfit_call(): pl.pallas_call(functools.partial(misfit_kernel, experts, tokens, slots),...  19.4 us
    pallas_call x1, Pallas kernels, solve_call(): pl.pallas_call(functools.partial(solve_kernel, group), grid=(tasks,), out...  17.2 us
    unnamed x14, local copies, waits for them, and re-layouts  3.82 us

profile of v1, /device:TPU:0, one launch (start us, length us, event | category | flops | bytes accessed | tf_op | source)
XLA Modules:
  0.0 79.4 jit_solution(2423975829743803985)
XLA Ops:
  0.6 0.0 copy-start
  0.6 0.0 copy-start.5
  0.7 0.0 copy-start.4
  0.7 37.1 %shard_map.77 = (bf16[768,768]{1,0:T(8,128)(2,1)}, bf16[768,768]{1,0:T(8,128)(2,1)}, f32[2]{0:T(128)}) custom-call(bf16[2,256,768]{2,1,0:T(8,128)(2,1)} %x_ref.1, s32[2,256]{1,0:T(2,128)} %routed_ref.1, bf16[4,768,256]{2,1,0:T(8,128)(2,1)} %w_ref.1), custom_call_target="tpu_custom_call" | custom-call | tf_op jit(solution)/shard_map/pallas_call | solution.py:186
  37.8 0.0 copy-done
  37.8 0.0 copy-done.5
  37.8 0.0 copy-done.4
  37.8 0.0 copy-start.1
  37.8 1.3 %copy-done.1 = bf16[768,768]{1,0:T(8,128)(2,1)S(1)} copy-done((bf16[768,768]{1,0:T(8,128)(2,1)S(1)}, bf16[768,768]{1,0:T(8,128)(2,1)}, u32[]{:S(2)}) %copy-start.1) | copy-done | bytes 1179672
  39.1 0.0 copy-start.2
  39.1 1.3 %copy-done.2 = bf16[768,768]{1,0:T(8,128)(2,1)S(1)} copy-done((bf16[768,768]{1,0:T(8,128)(2,1)S(1)}, bf16[768,768]{1,0:T(8,128)(2,1)}, u32[]{:S(2)}) %copy-start.2) | copy-done | bytes 1179672
  40.3 0.0 copy-start.6
  40.3 0.7 copy-done.6
  41.0 17.2 %shard_map.78 = (f32[4,768,256]{2,1,0:T(8,128)}, f32[8,128]{1,0:T(8,128)S(1)}) custom-call(s32[4]{0:T(128)S(1)} %copy-done.4, f32[4]{0:T(128)S(1)} %copy-done.5, f32[2]{0:T(128)S(1)} %copy-done.6, bf16[768,768]{1,0:T(8,128)(2,1)S(1)} %copy-done.1, bf16[768,768]{1,0:T(8,128)(2,1)S(1)} %copy-done.2, bf16[4,768,256]{2,1,0:T(8,128)(2,1)S(1)} %copy-done, ...), custom_call_target="tpu_custom_call" | custom-call | tf_op jit(solution)/shard_map/pallas_call | solution.py:290
  58.3 0.0 copy-start.3
  58.3 0.6 copy-done.3
  58.9 19.4 %shard_map.79 = f32[1,128]{1,0:T(1,128)} custom-call(f32[8,128]{1,0:T(8,128)} %copy-done.3), custom_call_target="tpu_custom_call" | custom-call | tf_op jit(solution)/shard_map/pallas_call | solution.py:352
  78.3 1.2 %slice_bitcast_fusion = f32[2]{0:T(128)} fusion(f32[1,128]{1,0:T(1,128)} %shard_map.79), kind=kLoop, calls=%fused_computation | loop fusion | bytes 16 | tf_op jit(solution)/shard_map/squeeze | solution.py:373
Async XLA Ops:
  0.6 37.1 %copy-start = (bf16[4,768,256]{2,1,0:T(8,128)(2,1)S(1)}, bf16[4,768,256]{2,1,0:T(8,128)(2,1)}, u32[]{:S(2)}) copy-start(bf16[4,768,256]{2,1,0:T(8,128)(2,1)} %w_ref.1) | copy-start | bytes 4718596
  0.6 37.1 %copy-start.5 = (f32[4]{0:T(128)S(1)}, f32[4]{0:T(128)}, u32[]{:S(2)}) copy-start(f32[4]{0:T(128)} %ridge_ref.1) | copy-start | bytes 52
  0.7 37.1 %copy-start.4 = (s32[4]{0:T(128)S(1)}, s32[4]{0:T(128)}, u32[]{:S(2)}) copy-start(s32[4]{0:T(128)} %counts_ref.1) | copy-start | bytes 52
  37.8 1.3 %copy-start.1 = (bf16[768,768]{1,0:T(8,128)(2,1)S(1)}, bf16[768,768]{1,0:T(8,128)(2,1)}, u32[]{:S(2)}) copy-start(bf16[768,768]{1,0:T(8,128)(2,1)} %get-tuple-element.8.high_ref) | copy-start | bytes 3538948
  39.1 1.3 %copy-start.2 = (bf16[768,768]{1,0:T(8,128)(2,1)S(1)}, bf16[768,768]{1,0:T(8,128)(2,1)}, u32[]{:S(2)}) copy-start(bf16[768,768]{1,0:T(8,128)(2,1)} %get-tuple-element.9.low_ref) | copy-start | bytes 3538948
  40.3 0.7 copy-start.6
  58.3 0.6 copy-start.3
